TPU v7x, 32 devices: a whole 2x2x4 slice. The times are simulated.
32 devices in a mesh: ctx: 4 (over z), tp: 4 (over y, x), dp: 2 (over core).
Axes of the slice: x: 2, y: 2, z: 4, core: 2. Of those that a mesh axis runs over, the one named last changes fastest.
Arguments:
- queries: bfloat16 [6144, 2048], P(('dp', 'ctx'), 'tp'), parts along dimension 0, may hold values from -6 to 6
- key_rows: bfloat16 [6144, 2048], P(('dp', 'ctx'), 'tp'), parts along dimension 0, may hold values from -6 to 6
- values: bfloat16 [6144, 2048], P(('dp', 'ctx'), 'tp'), parts along dimension 0, may hold values from -6 to 6
- doc_lengths: int32 [16], P('dp'), parts along dimension 0, may hold values from 1 to 2304, 3072 in all
- in_gate: bfloat16 [6144, 2048], P(('dp', 'ctx'), 'tp'), parts along dimension 0, may hold values from -6 to 6
- out_gate: bfloat16 [6144, 2048], P(('dp', 'ctx'), 'tp'), parts along dimension 0, may hold values from -6 to 6
- filter_taps: float32 [4096, 3072], P(('dp', 'tp'), 'ctx'), parts along dimension 0, may hold values from -0.21875 to 0.21875
Outputs:
- attn_out: bfloat16 [6144, 2048], P(('dp', 'ctx'), 'tp'), parts along dimension 0
- hyena_out: bfloat16 [6144, 2048], P(('dp', 'ctx'), 'tp'), parts along dimension 0
There are 2 independent parts, one for each index of `dp`. A program takes and returns all parts, laid end to end along the dimension named above; each array names one. Nothing has to cross between parts.
Inputs may be any that keep to these rules, and one draw needn't show every extreme that they name: `doc_lengths`: the lengths sum to 3072, and the longest is exactly 2304.
All inputs are finite; a program needn't handle non-finite values.
Results may differ from a plain program's by a relative error of at most 0.012.
Values may be sent and summed in bfloat16 or wider, within the bound.
A program may use at most 192 MiB of HBM per device.

v0:
```python
import math

import jax
import jax.numpy as jnp
import numpy as np
from jax import lax
from jax.experimental import pallas as pl
from jax.experimental.pallas import tpu as pltpu
from jax.sharding import PartitionSpec as P

HEAD_DIM = 128
KV_REACH = 3
BLOCK = 256


masked_score = -1e30


def passed_along(x, axis, by):
    length = lax.axis_size(axis)
    pairs = [(i, i + by) for i in range(length) if 0 <= i + by < length]
    return lax.ppermute(x, axis, pairs)


def doc_of(positions, doc_lengths):
    starts = jnp.cumsum(doc_lengths) - doc_lengths
    inside = (starts[None, :] <= positions[:, None]).astype(jnp.int32)
    return jnp.sum(inside, axis=1) - 1


def attend_block(carried, pair, query_heads, allowed):
    running_max, running_sum, weighted = carried
    row_count = query_heads.shape[0]
    key_heads = pair[0].reshape(row_count, -1, HEAD_DIM)
    value_heads = pair[1].reshape(row_count, -1, HEAD_DIM)
    scores = jnp.einsum(
        "qhd,khd->hqk", query_heads, key_heads, preferred_element_type=jnp.float32
    ) / math.sqrt(HEAD_DIM)
    scores = jnp.where(allowed[None], scores, masked_score)
    new_max = jnp.maximum(running_max, jnp.max(scores, axis=2))
    rescale = jnp.exp(running_max - new_max)
    exp_scores = jnp.exp(scores - new_max[:, :, None])
    running_sum = running_sum * rescale + jnp.sum(exp_scores, axis=2)
    weighted = weighted * rescale[:, :, None] + jnp.einsum(
        "hqk,khd->hqd",
        exp_scores.astype(jnp.bfloat16),
        value_heads,
        preferred_element_type=jnp.float32,
    )
    return (new_max, running_sum, weighted)


def split_parts(source):
    high_part = lax.optimization_barrier(source.astype(jnp.bfloat16))
    low_part = (source - high_part.astype(jnp.float32)).astype(jnp.bfloat16)
    return (high_part, low_part)


def split_mul(form, left_parts, right_parts):
    first = jnp.einsum(form, left_parts[0], right_parts[0], preferred_element_type=jnp.float32)
    second = jnp.einsum(form, left_parts[0], right_parts[1], preferred_element_type=jnp.float32)
    third = jnp.einsum(form, left_parts[1], right_parts[0], preferred_element_type=jnp.float32)
    return first + (second + third)


def dft_tables(length):
    inner_len = math.gcd(length, 256)
    outer_len = 2 * length // inner_len
    freq_rows = jnp.arange(outer_len, dtype=jnp.int32)
    time_rows = jnp.arange(outer_len // 2, dtype=jnp.int32)
    inner_index = jnp.arange(inner_len, dtype=jnp.int32)
    angle_outer = (
        2.0
        * math.pi
        / outer_len
        * (freq_rows[:, None] * time_rows[None, :] % outer_len).astype(jnp.float32)
    )
    angle_twist = (
        2.0
        * math.pi
        / (2 * length)
        * (freq_rows[:, None] * inner_index[None, :] % (2 * length)).astype(jnp.float32)
    )
    angle_inner = (
        2.0
        * math.pi
        / inner_len
        * (inner_index[:, None] * inner_index[None, :] % inner_len).astype(jnp.float32)
    )
    return (
        split_parts(jnp.cos(angle_outer)),
        split_parts(-jnp.sin(angle_outer)),
        jnp.cos(angle_twist),
        -jnp.sin(angle_twist),
        split_parts(jnp.cos(angle_inner)),
        split_parts(-jnp.sin(angle_inner)),
    )


def right_mul(left_parts, table_parts):
    return split_mul("cin,nm->cim", left_parts, table_parts)


def forward_dft(samples, tables):
    outer_cos, outer_sin, twist_cos, twist_sin, inner_cos, inner_sin = tables
    item_count = samples.shape[0]
    shaped = split_parts(samples.reshape(item_count, outer_cos[0].shape[1], inner_cos[0].shape[0]))
    section_real = split_mul("ij,cjn->cin", outer_cos, shaped)
    section_imag = split_mul("ij,cjn->cin", outer_sin, shaped)
    turned_real = split_parts(section_real * twist_cos - section_imag * twist_sin)
    turned_imag = split_parts(section_real * twist_sin + section_imag * twist_cos)
    spec_real = right_mul(turned_real, inner_cos) - right_mul(turned_imag, inner_sin)
    spec_imag = right_mul(turned_real, inner_sin) + right_mul(turned_imag, inner_cos)
    return (spec_real, spec_imag)


def inverse_dft(prod_real, prod_imag, tables):
    outer_cos, outer_sin, twist_cos, twist_sin, inner_cos, inner_sin = tables
    item_count = prod_real.shape[0]
    half_len = outer_cos[0].shape[1]
    inner_len = inner_cos[0].shape[0]
    real_parts = split_parts(prod_real)
    imag_parts = split_parts(prod_imag)
    back_real = right_mul(real_parts, inner_cos) + right_mul(imag_parts, inner_sin)
    back_imag = right_mul(imag_parts, inner_cos) - right_mul(real_parts, inner_sin)
    unturn_real = split_parts(back_real * twist_cos + back_imag * twist_sin)
    unturn_imag = split_parts(back_imag * twist_cos - back_real * twist_sin)
    rows_out = split_mul("ij,cin->cjn", outer_cos, unturn_real) + split_mul(
        "ij,cin->cjn", outer_sin, unturn_imag
    )
    return (rows_out * (1.0 / (2 * half_len * inner_len))).reshape(item_count, half_len * inner_len)


def filter_apply(signal, filter_spec, tables):
    sig_real, sig_imag = forward_dft(signal, tables)
    tap_real, tap_imag = filter_spec
    prod_real = sig_real * tap_real - sig_imag * tap_imag
    prod_imag = sig_real * tap_imag + sig_imag * tap_real
    return inverse_dft(prod_real, prod_imag, tables)


def body(queries, key_rows, values, doc_lengths, in_gate, out_gate, filter_taps):
    row_count, channels = queries.shape
    head_count = channels // HEAD_DIM
    group_count = lax.axis_size("ctx")
    per_group = channels // group_count
    seq_len = row_count * group_count
    tables = dft_tables(seq_len)
    taps_grouped = filter_taps.reshape(group_count, per_group, row_count)
    query_pos = lax.axis_index("ctx") * row_count + jnp.arange(row_count, dtype=jnp.int32)
    query_doc = doc_of(query_pos, doc_lengths)
    query_heads = queries.reshape(row_count, head_count, HEAD_DIM)
    carried = (
        jnp.full((head_count, row_count), masked_score, jnp.float32),
        jnp.zeros((head_count, row_count), jnp.float32),
        jnp.zeros((head_count, row_count, HEAD_DIM), jnp.float32),
    )

    def visit(state_now, pair, distance):
        key_pos = query_pos - distance * row_count
        key_doc = doc_of(key_pos, doc_lengths)
        allowed = (key_doc[None, :] == query_doc[:, None]) & (
            key_pos[None, :] <= query_pos[:, None]
        )
        return lax.cond(
            jnp.any(allowed),
            lambda state_in: attend_block(state_in, pair, query_heads, allowed),
            lambda state_in: state_in,
            state_now,
        )

    own_pair = jnp.stack((key_rows, values))
    carried = visit(carried, own_pair, 0)
    moving = own_pair
    for distance in range(1, KV_REACH + 1):
        moving = passed_along(moving, "ctx", 1)
        carried = visit(carried, moving, distance)
    running_max, running_sum, weighted = carried
    attended = (
        (weighted / running_sum[:, :, None])
        .transpose(1, 0, 2)
        .reshape(row_count, channels)
        .astype(jnp.bfloat16)
    )
    gated = (in_gate.astype(jnp.float32) * attended.astype(jnp.float32)).T
    gated_grouped = gated.reshape(group_count, per_group, row_count)
    pair = (
        lax.all_to_all(
            gated_grouped.astype(jnp.bfloat16), "ctx", split_axis=0, concat_axis=2, tiled=True
        ).astype(gated_grouped.dtype),
        lax.all_to_all(
            taps_grouped.astype(jnp.bfloat16), "ctx", split_axis=0, concat_axis=2, tiled=True
        ).astype(taps_grouped.dtype),
    )
    item_count = pair[0].shape[1]
    signal = pair[0].reshape(item_count, -1)
    taps = pair[1].reshape(item_count, -1)
    result = filter_apply(signal, forward_dft(taps, tables), tables)
    mixed = result.reshape(1, item_count, -1)
    returned = lax.all_to_all(
        mixed.astype(jnp.bfloat16), "ctx", split_axis=2, concat_axis=0, tiled=True
    ).astype(mixed.dtype)
    hyena_out = (out_gate.astype(jnp.float32) * returned.reshape(channels, row_count).T).astype(
        jnp.bfloat16
    )
    return (attended, hyena_out)


def block_tables(block):
    freq = np.arange(block)
    time = np.arange(block)
    angle = np.pi / (2 * block) * ((2 * freq[:, None] + 1) * time[None, :] % (4 * block))
    forward = np.concatenate((np.cos(angle), -np.sin(angle)), axis=0)
    inverse = forward.T / block
    return (jnp.asarray(forward, jnp.bfloat16), jnp.asarray(inverse, jnp.bfloat16))


def fused_kernel(
    docs_ref,
    query_ref,
    key_ref,
    value_ref,
    gate_ref,
    taps_ref,
    out_gate_ref,
    forward_ref,
    inverse_ref,
    attn_ref,
    hyena_ref,
    all_query,
    all_key,
    all_value,
    all_gate,
    all_taps,
    own_out_gate,
    score_buf,
    attn_buf,
    sig_spec,
    tap_spec,
    prod_spec,
    mixed_buf,
    mixed_back,
    send_sem,
    recv_sem,
    local_sem,
):
    rows, _ = query_ref.shape
    length, width = all_query.shape
    groups = length // rows
    block = inverse_ref.shape[0]
    blocks = length // block
    per_row = rows // block
    reach = KV_REACH * per_row
    me = lax.axis_index("ctx")

    def rows_of(group):
        return pl.ds(pl.multiple_of(group * rows, rows), rows)

    def cols_of(group):
        return pl.ds(pl.multiple_of(group * width, width), width)

    barrier = pltpu.get_barrier_semaphore()
    for step in range(1, groups):
        peer = lax.rem(me + step, groups)
        pl.semaphore_signal(
            barrier, inc=1, device_id={"ctx": peer}, device_id_type=pl.DeviceIdType.MESH
        )
    pl.semaphore_wait(barrier, groups - 1)

    def remote(source, target, kind, step):
        return pltpu.make_async_remote_copy(
            src_ref=source,
            dst_ref=target,
            send_sem=send_sem.at[kind, step],
            recv_sem=recv_sem.at[kind, step],
            device_id={"ctx": lax.rem(me + step, groups)},
            device_id_type=pl.DeviceIdType.MESH,
        )

    def inbound(kind, step):
        peer = lax.rem(me + step, groups)
        source_of = (query_ref, key_ref, value_ref, gate_ref)
        target_of = (all_query, all_key, all_value, all_gate)
        if kind == 4:
            return (
                taps_ref.at[rows_of_width(peer), :],
                all_taps.at[:, rows_of(me)],
            )
        return (source_of[kind].at[:, cols_of(peer)], target_of[kind].at[rows_of(me), :])

    def rows_of_width(group):
        return pl.ds(pl.multiple_of(group * width, width), width)

    sends = {}
    own = {}
    for kind in range(5):
        for step in range(1, groups):
            source, target = inbound(kind, step)
            sends[kind, step] = remote(source, target, kind, step)
            sends[kind, step].start()
    for kind in range(5):
        source, target = inbound(kind, 0)
        own[kind] = pltpu.make_async_copy(source, target, local_sem.at[kind])
        own[kind].start()
    gate_copy = pltpu.make_async_copy(out_gate_ref, own_out_gate, local_sem.at[5])
    gate_copy.start()

    def arrive(kind):
        own[kind].wait()
        for step in range(1, groups):
            sends[kind, step].wait_recv()

    starts = []
    total = jnp.int32(0)
    for doc in range(docs_ref.shape[0]):
        starts.append(total)
        total = total + docs_ref[doc]

    for kind in range(3):
        arrive(kind)

    def query_tile(tile):
        low = jnp.maximum(tile - reach, 0)
        row0 = pl.multiple_of(tile * block, block)
        query = all_query[pl.ds(row0, block), :]
        row_pos = lax.broadcasted_iota(jnp.int32, (block, width), 0) + tile * block
        row_start = jnp.zeros((block, width), jnp.int32)
        for start in starts:
            row_start = jnp.where(row_pos >= start, start, row_start)
        row_pos = row_pos[:, :1]
        row_start = row_start[:, :1]
        lane_pos = lax.broadcasted_iota(jnp.int32, (block, block), 1)

        def score_step(at, top):
            key = all_key[pl.ds(pl.multiple_of(at * block, block), block), :]
            scores = lax.dot_general(
                query, key, (((1,), (1,)), ((), ())), preferred_element_type=jnp.float32
            ) * (1.0 / math.sqrt(HEAD_DIM))
            key_pos = lane_pos + at * block
            allowed = (key_pos <= row_pos) & (key_pos >= row_start)
            scores = jnp.where(allowed, scores, masked_score)
            score_buf[at - low] = scores
            for part in range(0, block, width):
                top = jnp.maximum(top, scores[:, part : part + width])
            return top

        top = lax.fori_loop(
            low, tile + 1, score_step, jnp.full((block, width), masked_score, jnp.float32)
        )
        top = jnp.max(top, axis=1, keepdims=True)

        def value_step(at, carried):
            running, weighted = carried
            value = all_value[pl.ds(pl.multiple_of(at * block, block), block), :]
            weight = jnp.exp(score_buf[at - low] - top)
            for part in range(0, block, width):
                running = running + weight[:, part : part + width]
            weighted = weighted + jnp.dot(
                weight.astype(jnp.bfloat16), value, preferred_element_type=jnp.float32
            )
            return (running, weighted)

        zero = jnp.zeros((block, width), jnp.float32)
        running, weighted = lax.fori_loop(low, tile + 1, value_step, (zero, zero))
        running = jnp.sum(running, axis=1, keepdims=True)
        attn_buf[pl.ds(row0, block), :] = (weighted / running).astype(jnp.bfloat16)

    def attn_send(step):
        peer = lax.rem(me + step, groups)
        sends[5, step] = remote(
            attn_buf.at[rows_of(peer), :], attn_ref.at[:, cols_of(me)], 5, step
        )
        sends[5, step].start()

    order = list(range(1, groups)) + [0]
    for place, step in enumerate(order):
        group = lax.rem(me + step, groups)

        def tile_body(at, carry, group=group):
            query_tile(group * per_row + at)
            return carry

        lax.fori_loop(0, per_row, tile_body, 0)
        if place > 0:
            attn_send(order[place - 1])

    arrive(4)

    def tap_body(at, carry):
        col0 = pl.multiple_of(at * block, block)
        tap_spec[at] = lax.dot_general(
            forward_ref[...],
            all_taps[:, pl.ds(col0, block)],
            (((1,), (1,)), ((), ())),
            preferred_element_type=jnp.float32,
        )
        return carry

    lax.fori_loop(0, blocks, tap_body, 0)
    own_attn = pltpu.make_async_copy(
        attn_buf.at[rows_of(me), :], attn_ref.at[:, cols_of(me)], local_sem.at[6]
    )
    own_attn.start()
    arrive(3)

    def signal_body(at, carry):
        row0 = pl.multiple_of(at * block, block)
        gated = all_gate[pl.ds(row0, block), :].astype(jnp.float32) * attn_buf[
            pl.ds(row0, block), :
        ].astype(jnp.float32)
        sig_spec[at] = jnp.dot(
            forward_ref[...], gated.astype(jnp.bfloat16), preferred_element_type=jnp.float32
        )
        return carry

    lax.fori_loop(0, blocks, signal_body, 0)

    lift = 8

    def product_body(at, carry):
        real = pl.ds(pl.multiple_of(at * lift, lift), lift)
        imag = pl.ds(pl.multiple_of(block + at * lift, lift), lift)
        odd = lax.rem(lax.broadcasted_iota(jnp.int32, (lift, width), 0), 2) == 1
        sign = jnp.where(odd, -1.0, 1.0).astype(jnp.float32)
        tap_real = []
        tap_imag = []
        for k in range(blocks):
            now_real = tap_spec[k, real, :]
            now_imag = tap_spec[k, imag, :]
            if k > 0:
                now_real = now_real - sign * tap_spec[k - 1, imag, :]
                now_imag = now_imag + sign * tap_spec[k - 1, real, :]
            tap_real.append(now_real)
            tap_imag.append(now_imag)
        for out in range(blocks):
            sum_real = jnp.zeros((lift, width), jnp.float32)
            sum_imag = jnp.zeros((lift, width), jnp.float32)
            for j in range(out + 1):
                sig_real = sig_spec[j, real, :]
                sig_imag = sig_spec[j, imag, :]
                sum_real = sum_real + sig_real * tap_real[out - j] - sig_imag * tap_imag[out - j]
                sum_imag = sum_imag + sig_real * tap_imag[out - j] + sig_imag * tap_real[out - j]
            prod_spec[out, real, :] = sum_real
            prod_spec[out, imag, :] = sum_imag
        return carry

    lax.fori_loop(0, block // lift, product_body, 0)

    def mixed_send(step):
        peer = lax.rem(me + step, groups)
        sends[6, step] = remote(
            mixed_buf.at[rows_of(peer), :], mixed_back.at[:, cols_of(me)], 6, step
        )
        sends[6, step].start()

    for place, step in enumerate(order):
        group = lax.rem(me + step, groups)

        def inverse_body(at, carry, group=group, step=step):
            index = group * per_row + at
            mixed = jnp.dot(
                inverse_ref[...],
                prod_spec[index].astype(jnp.bfloat16),
                preferred_element_type=jnp.float32,
            ).astype(jnp.bfloat16)
            if step == 0:
                mixed_back[pl.ds(pl.multiple_of(at * block, block), block), cols_of(me)] = mixed
            else:
                mixed_buf[pl.ds(pl.multiple_of(index * block, block), block), :] = mixed
            return carry

        lax.fori_loop(0, per_row, inverse_body, 0)
        if place > 0:
            mixed_send(order[place - 1])

    gate_copy.wait()
    for step in range(1, groups):
        sends[6, step].wait_recv()

    def final_body(at, carry):
        part = pl.ds(pl.multiple_of(at * 64, 64), 64)
        hyena_ref[part, :] = (
            own_out_gate[part, :].astype(jnp.float32) * mixed_back[part, :].astype(jnp.float32)
        ).astype(jnp.bfloat16)
        return carry

    lax.fori_loop(0, rows // 64, final_body, 0)
    own_attn.wait()
    for step in range(1, groups):
        sends[5, step].wait_recv()
    for copy in sends.values():
        copy.wait_send()


def fused_body(queries, key_rows, values, doc_lengths, in_gate, out_gate, filter_taps):
    rows, channels = queries.shape
    groups = lax.axis_size("ctx")
    width = channels // groups
    length = rows * groups
    block = BLOCK
    blocks = length // block
    reach = KV_REACH * (rows // block)
    forward, inverse = block_tables(block)
    anywhere = pl.BlockSpec(memory_space=pl.ANY)
    vmem = pl.BlockSpec(memory_space=pltpu.VMEM)
    half = jnp.bfloat16
    full = jnp.float32
    return pl.pallas_call(
        fused_kernel,
        out_shape=(
            jax.ShapeDtypeStruct((rows, channels), half),
            jax.ShapeDtypeStruct((rows, channels), half),
        ),
        in_specs=[pl.BlockSpec(memory_space=pltpu.SMEM)] + [anywhere] * 6 + [vmem] * 2,
        out_specs=(anywhere, vmem),
        scratch_shapes=[
            pltpu.VMEM((length, width), half),
            pltpu.VMEM((length, width), half),
            pltpu.VMEM((length, width), half),
            pltpu.VMEM((length, width), half),
            pltpu.VMEM((width, length), half),
            pltpu.VMEM((rows, channels), half),
            pltpu.VMEM((min(reach + 1, blocks), block, block), full),
            pltpu.VMEM((length, width), half),
            pltpu.VMEM((blocks, 2 * block, width), full),
            pltpu.VMEM((blocks, 2 * block, width), full),
            pltpu.VMEM((blocks, 2 * block, width), full),
            pltpu.VMEM((length, width), half),
            pltpu.VMEM((rows, channels), half),
            pltpu.SemaphoreType.DMA((7, groups)),
            pltpu.SemaphoreType.DMA((7, groups)),
            pltpu.SemaphoreType.DMA((7,)),
        ],
        compiler_params=pltpu.CompilerParams(
            collective_id=0, has_side_effects=True, vmem_limit_bytes=48 * 1024 * 1024
        ),
        name="fused_window",
    )(
        doc_lengths,
        queries,
        key_rows,
        values,
        in_gate,
        filter_taps.astype(half),
        out_gate,
        forward,
        inverse,
    )


def fits_fused(queries):
    rows, channels = queries.shape
    groups = lax.axis_size("ctx")
    return channels == groups * HEAD_DIM and rows % BLOCK == 0


def either_body(queries, *rest):
    if fits_fused(queries):
        return fused_body(queries, *rest)
    return body(queries, *rest)


def solution(mesh):
    return jax.shard_map(
        either_body,
        mesh=mesh,
        in_specs=(
            P(("dp", "ctx"), "tp"),
            P(("dp", "ctx"), "tp"),
            P(("dp", "ctx"), "tp"),
            P("dp"),
            P(("dp", "ctx"), "tp"),
            P(("dp", "ctx"), "tp"),
            P(("dp", "tp"), "ctx"),
        ),
        out_specs=(P(("dp", "ctx"), "tp"), P(("dp", "ctx"), "tp")),
        check_vma=False,
    )
```

profile of v0, /device:TPU:24, one launch (start us, length us, event | category | flops | bytes accessed | tf_op | source)
XLA Modules:
  0.0 143.2 jit_solution(15693745788589756951)
XLA Ops:
  0.6 0.0 copy-start.2
  0.6 0.0 copy-start.1
  0.7 0.0 copy-start
  0.7 1.6 %convert_element_type.3.taps_ref = bf16[512,768]{1,0:T(8,128)(2,1)S(1)} convert(f32[512,768]{1,0:T(8,128)} %param.15) | non-fusion elementwise | flops 393216 | bytes 2359296 | tf_op jit(solution)/shard_map/convert_element_type | solution.py:544
  2.3 0.0 copy-done.2
  2.3 0.2 copy-done.1
  2.5 0.2 copy-done
  2.7 0.0 copy-start.3
  2.7 1.1 copy-done.3
  3.8 0.0 copy-start.4
  3.9 0.9 copy-done.4
  4.8 0.0 copy-start.5
  4.8 0.9 copy-done.5
  5.7 0.0 copy-start.6
  5.8 0.7 copy-done.6
  6.4 135.0 %fused_window.1 = (bf16[768,512]{1,0:T(8,128)(2,1)S(1)}, bf16[768,512]{1,0:T(8,128)(2,1)S(1)}) custom-call(s32[8]{0:T(128)S(1)} %copy-done.6, bf16[768,512]{1,0:T(8,128)(2,1)S(1)} %copy-done, bf16[768,512]{1,0:T(8,128)(2,1)S(1)} %copy-done.1, bf16[768,512]{1,0:T(8,128)(2,1)S(1)} %copy-done.2, bf16[768,512]{1,0:T(8,128)(2,1)S(1)} %copy-done.3, ...), custom_call_target="tpu_custom_call" | custom-call | tf_op jit(solution)/shard_map/fused_window/pallas_call | solution.py:508
  141.4 0.9 copy.13
  142.3 0.9 copy.14
Async XLA Ops:
  0.6 1.7 %copy-start.2 = (bf16[768,512]{1,0:T(8,128)(2,1)S(1)}, bf16[768,512]{1,0:T(8,128)(2,1)}, u32[]{:S(2)}) copy-start(bf16[768,512]{1,0:T(8,128)(2,1)} %value_ref.1) | copy-start | bytes 2359300
  0.6 1.8 %copy-start.1 = (bf16[768,512]{1,0:T(8,128)(2,1)S(1)}, bf16[768,512]{1,0:T(8,128)(2,1)}, u32[]{:S(2)}) copy-start(bf16[768,512]{1,0:T(8,128)(2,1)} %key_ref.1) | copy-start | bytes 2359300
  0.7 2.1 %copy-start = (bf16[768,512]{1,0:T(8,128)(2,1)S(1)}, bf16[768,512]{1,0:T(8,128)(2,1)}, u32[]{:S(2)}) copy-start(bf16[768,512]{1,0:T(8,128)(2,1)} %query_ref.1) | copy-start | bytes 2359300
  2.7 1.1 copy-start.3
  3.8 0.9 copy-start.4
  4.8 0.9 copy-start.5
  5.7 0.7 copy-start.6
where the time goes:
time: 143 us
  Pallas kernels  135 us (94%)
  local copies, waits for them, and re-layouts  5.86 us (4%)
  other arithmetic  1.64 us (1%)
    pallas_call x1, Pallas kernels, fused_body(): pl.pallas_call(fused_kernel, out_shape=(jax.ShapeDtypeStruct((rows, chann...  135 us
    unnamed x16, local copies, waits for them, and re-layouts  5.86 us

commit v1 on v0

--- a/solution.py
+++ b/solution.py
@@ -227,6 +227,16 @@
     inverse_ref,
     attn_ref,
     hyena_ref,
+    near_query,
+    near_key,
+    near_value,
+    near_gate,
+    near_attn,
+    near_gated,
+    wide_taps,
+    half_taps,
+    forward_buf,
+    inverse_buf,
     all_query,
     all_key,
     all_value,
@@ -243,15 +253,19 @@
     send_sem,
     recv_sem,
     local_sem,
+    table_sem,
 ):
     rows, _ = query_ref.shape
     length, width = all_query.shape
     groups = length // rows
     block = inverse_ref.shape[0]
+    half = groups // 2
+    half_cols = pl.ds(half * width, width * (groups - half))
     blocks = length // block
     per_row = rows // block
     reach = KV_REACH * per_row
     me = lax.axis_index("ctx")
+    lower = me < half
 
     def rows_of(group):
         return pl.ds(pl.multiple_of(group * rows, rows), rows)
@@ -267,15 +281,35 @@
         )
     pl.semaphore_wait(barrier, groups - 1)
 
-    def remote(source, target, kind, step):
-        return pltpu.make_async_remote_copy(
-            src_ref=source,
-            dst_ref=target,
-            send_sem=send_sem.at[kind, step],
-            recv_sem=recv_sem.at[kind, step],
-            device_id={"ctx": lax.rem(me + step, groups)},
-            device_id_type=pl.DeviceIdType.MESH,
-        )
+    class Later:
+        def __init__(self, make):
+            self.make = make
+
+        def start(self):
+            self.make().start()
+
+        def wait(self):
+            self.make().wait()
+
+        def wait_recv(self):
+            self.make().wait_recv()
+
+        def wait_send(self):
+            self.make().wait_send()
+
+    def remote(refs, kind, step):
+        def make():
+            source, target = refs()
+            return pltpu.make_async_remote_copy(
+                src_ref=source,
+                dst_ref=target,
+                send_sem=send_sem.at[kind, step],
+                recv_sem=recv_sem.at[kind, step],
+                device_id={"ctx": lax.rem(me + step, groups)},
+                device_id_type=pl.DeviceIdType.MESH,
+            )
+
+        return Later(make)
 
     def inbound(kind, step):
         peer = lax.rem(me + step, groups)
@@ -283,46 +317,89 @@
         target_of = (all_query, all_key, all_value, all_gate)
         if kind == 4:
             return (
-                taps_ref.at[rows_of_width(peer), :],
+                half_taps.at[cols_of(peer), :],
                 all_taps.at[:, rows_of(me)],
             )
         return (source_of[kind].at[:, cols_of(peer)], target_of[kind].at[rows_of(me), :])
 
-    def rows_of_width(group):
-        return pl.ds(pl.multiple_of(group * width, width), width)
+    def goes(kind, source, target):
+        if kind == 0:
+            return (source >= half) | (target < half)
+        if kind == 5:
+            return (source < half) | (target >= half)
+        return None
+
+    def guarded(condition, action):
+        if condition is None:
+            action()
+        else:
+            pl.when(condition)(action)
 
     sends = {}
     own = {}
-    for kind in range(5):
+
+    def make_send(kind, step):
+        sends[kind, step] = remote(lambda: inbound(kind, step), kind, step)
+
+    def near_copy(kind, step):
+        source = (key_ref, value_ref)[kind - 7]
+        target = (near_key, near_value)[kind - 7]
+        return remote(
+            lambda: (source.at[:, half_cols], target.at[rows_of(me), :]), kind, step
+        )
+
+    def own_copy(refs, place):
+        def make():
+            source, target = refs()
+            return pltpu.make_async_copy(source, target, table_sem.at[place])
+
+        own[place] = Later(make)
+        own[place].start()
+
+    for kind in (7, 8):
+        for step in range(1, half):
+            sends[kind, step] = near_copy(kind, step)
+            pl.when(me + step < half)(sends[kind, step].start)
+    for kind in range(4):
         for step in range(1, groups):
-            source, target = inbound(kind, step)
-            sends[kind, step] = remote(source, target, kind, step)
-            sends[kind, step].start()
-    for kind in range(5):
+            make_send(kind, step)
+            peer = lax.rem(me + step, groups)
+            guarded(
+                goes(0, me, peer) if kind in (0, 3) else None, sends[kind, step].start
+            )
+
+    @pl.when(lower)
+    def _():
+        own_copy(lambda: (query_ref.at[:, half_cols], near_query), 0)
+        own_copy(lambda: (key_ref.at[:, half_cols], near_key.at[rows_of(me), :]), 1)
+        own_copy(lambda: (value_ref.at[:, half_cols], near_value.at[rows_of(me), :]), 2)
+        own_copy(lambda: (gate_ref.at[:, half_cols], near_gate), 3)
+
+    own_copy(lambda: (taps_ref, wide_taps), 4)
+    own_copy(lambda: (forward_ref, forward_buf), 5)
+    own_copy(lambda: (inverse_ref, inverse_buf), 6)
+    local = {}
+    for kind in range(4):
         source, target = inbound(kind, 0)
-        own[kind] = pltpu.make_async_copy(source, target, local_sem.at[kind])
-        own[kind].start()
+        local[kind] = pltpu.make_async_copy(source, target, local_sem.at[kind])
+        local[kind].start()
     gate_copy = pltpu.make_async_copy(out_gate_ref, own_out_gate, local_sem.at[5])
     gate_copy.start()
 
     def arrive(kind):
-        own[kind].wait()
+        local[kind].wait()
         for step in range(1, groups):
-            sends[kind, step].wait_recv()
+            source = lax.rem(me + groups - step, groups)
+            guarded(goes(kind, source, me), sends[kind, step].wait_recv)
 
     starts = []
-    total = jnp.int32(0)
+    total = 0
     for doc in range(docs_ref.shape[0]):
         starts.append(total)
         total = total + docs_ref[doc]
 
-    for kind in range(3):
-        arrive(kind)
-
-    def query_tile(tile):
+    def query_tile(tile, query, key_of, value_of):
         low = jnp.maximum(tile - reach, 0)
-        row0 = pl.multiple_of(tile * block, block)
-        query = all_query[pl.ds(row0, block), :]
         row_pos = lax.broadcasted_iota(jnp.int32, (block, width), 0) + tile * block
         row_start = jnp.zeros((block, width), jnp.int32)
         for start in starts:
@@ -332,7 +409,7 @@
         lane_pos = lax.broadcasted_iota(jnp.int32, (block, block), 1)
 
         def score_step(at, top):
-            key = all_key[pl.ds(pl.multiple_of(at * block, block), block), :]
+            key = key_of(pl.ds(pl.multiple_of(at * block, block), block))
             scores = lax.dot_general(
                 query, key, (((1,), (1,)), ((), ())), preferred_element_type=jnp.float32
             ) * (1.0 / math.sqrt(HEAD_DIM))
@@ -351,7 +428,7 @@
 
         def value_step(at, carried):
             running, weighted = carried
-            value = all_value[pl.ds(pl.multiple_of(at * block, block), block), :]
+            value = value_of(pl.ds(pl.multiple_of(at * block, block), block))
             weight = jnp.exp(score_buf[at - low] - top)
             for part in range(0, block, width):
                 running = running + weight[:, part : part + width]
@@ -363,33 +440,112 @@
         zero = jnp.zeros((block, width), jnp.float32)
         running, weighted = lax.fori_loop(low, tile + 1, value_step, (zero, zero))
         running = jnp.sum(running, axis=1, keepdims=True)
-        attn_buf[pl.ds(row0, block), :] = (weighted / running).astype(jnp.bfloat16)
+        return (weighted / running).astype(jnp.bfloat16)
+
+    def near_send(head):
+        for step in range(1, groups):
+            peer = lax.rem(me + step, groups)
+
+            @pl.when(lower & (peer == half + head))
+            def _(step=step):
+                remote(
+                    lambda: (
+                        near_gated.at[:, pl.ds(head * width, width)],
+                        all_gate.at[rows_of(me), :],
+                    ),
+                    3,
+                    step,
+                ).start()
+
+    @pl.when(lower)
+    def _():
+        for place in range(4):
+            own[place].wait()
+        for kind in (7, 8):
+            for step in range(1, half):
+                pl.when(me - step >= 0)(sends[kind, step].wait_recv)
+        for head in range(groups - half):
+            cols = pl.ds(head * width, width)
+
+            def near_body(at, carry, cols=cols):
+                part = pl.ds(pl.multiple_of(at * block, block), block)
+                attended = query_tile(
+                    me * per_row + at,
+                    near_query[part, cols],
+                    lambda rows_at: near_key[rows_at, cols],
+                    lambda rows_at: near_value[rows_at, cols],
+                )
+                near_attn[part, cols] = attended
+                near_gated[part, cols] = (
+                    near_gate[part, cols].astype(jnp.float32) * attended.astype(jnp.float32)
+                ).astype(jnp.bfloat16)
+                return carry
+
+            lax.fori_loop(0, per_row, near_body, 0)
+            if head > 0:
+                near_send(head - 1)
+
+    own[4].wait()
+
+    def round_body(at, carry):
+        part = pl.ds(pl.multiple_of(at * 64, 64), 64)
+        half_taps[part, :] = wide_taps[part, :].astype(jnp.bfloat16)
+        return carry
+
+    lax.fori_loop(0, half_taps.shape[0] // 64, round_body, 0)
+    near_send(groups - half - 1)
+    near_out = Later(
+        lambda: pltpu.make_async_copy(near_attn, attn_ref.at[:, half_cols], table_sem.at[7])
+    )
+    pl.when(lower)(near_out.start)
+
+    arrive(0)
+    for step in range(1, groups):
+        make_send(4, step)
+        sends[4, step].start()
+    source, target = inbound(4, 0)
+    local[4] = pltpu.make_async_copy(source, target, local_sem.at[4])
+    local[4].start()
+    arrive(1)
+    arrive(2)
 
     def attn_send(step):
         peer = lax.rem(me + step, groups)
         sends[5, step] = remote(
-            attn_buf.at[rows_of(peer), :], attn_ref.at[:, cols_of(me)], 5, step
+            lambda: (attn_buf.at[rows_of(peer), :], attn_ref.at[:, cols_of(me)]), 5, step
         )
-        sends[5, step].start()
+        guarded(goes(5, me, peer), sends[5, step].start)
 
     order = list(range(1, groups)) + [0]
     for place, step in enumerate(order):
         group = lax.rem(me + step, groups)
 
         def tile_body(at, carry, group=group):
-            query_tile(group * per_row + at)
+            tile = group * per_row + at
+            part = pl.ds(pl.multiple_of(tile * block, block), block)
+            attn_buf[part, :] = query_tile(
+                tile,
+                all_query[part, :],
+                lambda rows_at: all_key[rows_at, :],
+                lambda rows_at: all_value[rows_at, :],
+            )
             return carry
 
-        lax.fori_loop(0, per_row, tile_body, 0)
+        @pl.when(goes(5, me, group))
+        def _(tile_body=tile_body):
+            lax.fori_loop(0, per_row, tile_body, 0)
+
         if place > 0:
             attn_send(order[place - 1])
 
     arrive(4)
+    own[5].wait()
+    own[6].wait()
 
     def tap_body(at, carry):
         col0 = pl.multiple_of(at * block, block)
         tap_spec[at] = lax.dot_general(
-            forward_ref[...],
+            forward_buf[...],
             all_taps[:, pl.ds(col0, block)],
             (((1,), (1,)), ((), ())),
             preferred_element_type=jnp.float32,
@@ -405,12 +561,11 @@
 
     def signal_body(at, carry):
         row0 = pl.multiple_of(at * block, block)
-        gated = all_gate[pl.ds(row0, block), :].astype(jnp.float32) * attn_buf[
-            pl.ds(row0, block), :
-        ].astype(jnp.float32)
-        sig_spec[at] = jnp.dot(
-            forward_ref[...], gated.astype(jnp.bfloat16), preferred_element_type=jnp.float32
-        )
+        arrived = all_gate[pl.ds(row0, block), :]
+        gated = arrived.astype(jnp.float32) * attn_buf[pl.ds(row0, block), :].astype(jnp.float32)
+        ready = (me >= half) & (at < half * per_row)
+        gated = jnp.where(ready, arrived, gated.astype(jnp.bfloat16))
+        sig_spec[at] = jnp.dot(forward_buf[...], gated, preferred_element_type=jnp.float32)
         return carry
 
     lax.fori_loop(0, blocks, signal_body, 0)
@@ -449,7 +604,7 @@
     def mixed_send(step):
         peer = lax.rem(me + step, groups)
         sends[6, step] = remote(
-            mixed_buf.at[rows_of(peer), :], mixed_back.at[:, cols_of(me)], 6, step
+            lambda: (mixed_buf.at[rows_of(peer), :], mixed_back.at[:, cols_of(me)]), 6, step
         )
         sends[6, step].start()
 
@@ -459,7 +614,7 @@
         def inverse_body(at, carry, group=group, step=step):
             index = group * per_row + at
             mixed = jnp.dot(
-                inverse_ref[...],
+                inverse_buf[...],
                 prod_spec[index].astype(jnp.bfloat16),
                 preferred_element_type=jnp.float32,
             ).astype(jnp.bfloat16)
@@ -486,10 +641,15 @@
 
     lax.fori_loop(0, rows // 64, final_body, 0)
     own_attn.wait()
+    pl.when(lower)(near_out.wait)
     for step in range(1, groups):
-        sends[5, step].wait_recv()
-    for copy in sends.values():
-        copy.wait_send()
+        source = lax.rem(me + groups - step, groups)
+        guarded(goes(5, source, me), sends[5, step].wait_recv)
+    for (kind, step), copy in sends.items():
+        if kind >= 7:
+            guarded(me + step < half, copy.wait_send)
+        else:
+            guarded(goes(kind, me, lax.rem(me + step, groups)), copy.wait_send)
 
 
 def fused_body(queries, key_rows, values, doc_lengths, in_gate, out_gate, filter_taps):
@@ -501,6 +661,8 @@
     blocks = length // block
     reach = KV_REACH * (rows // block)
     forward, inverse = block_tables(block)
+    near = groups // 2
+    far = (groups - near) * width
     anywhere = pl.BlockSpec(memory_space=pl.ANY)
     vmem = pl.BlockSpec(memory_space=pltpu.VMEM)
     half = jnp.bfloat16
@@ -511,9 +673,19 @@
             jax.ShapeDtypeStruct((rows, channels), half),
             jax.ShapeDtypeStruct((rows, channels), half),
         ),
-        in_specs=[pl.BlockSpec(memory_space=pltpu.SMEM)] + [anywhere] * 6 + [vmem] * 2,
+        in_specs=[pl.BlockSpec(memory_space=pltpu.SMEM)] + [anywhere] * 8,
         out_specs=(anywhere, vmem),
         scratch_shapes=[
+            pltpu.VMEM((rows, far), half),
+            pltpu.VMEM((near * rows, far), half),
+            pltpu.VMEM((near * rows, far), half),
+            pltpu.VMEM((rows, far), half),
+            pltpu.VMEM((rows, far), half),
+            pltpu.VMEM((rows, far), half),
+            pltpu.VMEM(filter_taps.shape, full),
+            pltpu.VMEM(filter_taps.shape, half),
+            pltpu.VMEM(forward.shape, half),
+            pltpu.VMEM(inverse.shape, half),
             pltpu.VMEM((length, width), half),
             pltpu.VMEM((length, width), half),
             pltpu.VMEM((length, width), half),
@@ -527,12 +699,13 @@
             pltpu.VMEM((blocks, 2 * block, width), full),
             pltpu.VMEM((length, width), half),
             pltpu.VMEM((rows, channels), half),
-            pltpu.SemaphoreType.DMA((7, groups)),
-            pltpu.SemaphoreType.DMA((7, groups)),
+            pltpu.SemaphoreType.DMA((9, groups)),
+            pltpu.SemaphoreType.DMA((9, groups)),
             pltpu.SemaphoreType.DMA((7,)),
+            pltpu.SemaphoreType.DMA((8,)),
         ],
         compiler_params=pltpu.CompilerParams(
-            collective_id=0, has_side_effects=True, vmem_limit_bytes=48 * 1024 * 1024
+            collective_id=0, has_side_effects=True, vmem_limit_bytes=67043328
         ),
         name="fused_window",
     )(
@@ -541,7 +714,7 @@
         key_rows,
         values,
         in_gate,
-        filter_taps.astype(half),
+        filter_taps,
         out_gate,
         forward,
         inverse,

time: 143 us -> 140 us (0.979)
  local copies, waits for them, and re-layouts: 5.86 us -> 3.02 us
  other arithmetic: 1.64 us -> 0 us
    unnamed x16 -> x4, local copies, waits for them, and re-layouts: 5.86 us -> 3.02 us
    convert_element_type x1 -> x0, other arithmetic: 1.64 us -> none  [fused_body(): filter_taps.astype(half)]
where the time goes in v1:
time: 140 us
  Pallas kernels  136 us (97%)
  local copies, waits for them, and re-layouts  3.02 us (2%)
    pallas_call x1, Pallas kernels, fused_body(): pl.pallas_call(fused_kernel, out_shape=(jax.ShapeDtypeStruct((rows, chann...  136 us
    unnamed x4, local copies, waits for them, and re-layouts  3.02 us

profile of v1, /device:TPU:24, one launch (start us, length us, event | category | flops | bytes accessed | tf_op | source)
XLA Modules:
  0.0 140.1 jit_solution(9297052761136565366)
XLA Ops:
  0.6 136.5 %fused_window.1 = (bf16[768,512]{1,0:T(8,128)(2,1)}, bf16[768,512]{1,0:T(8,128)(2,1)}) custom-call(s32[8]{0:T(128)} %docs_ref.1, bf16[768,512]{1,0:T(8,128)(2,1)} %query_ref.1, bf16[768,512]{1,0:T(8,128)(2,1)} %key_ref.1, bf16[768,512]{1,0:T(8,128)(2,1)} %value_ref.1, bf16[768,512]{1,0:T(8,128)(2,1)} %gate_ref.1, f32[512,768]{1,0:T(8,128)} %taps_ref.1, ...), custom_call_target="tpu_custom_call" | custom-call | tf_op jit(solution)/shard_map/fused_window/pallas_call | solution.py:670
  137.1 0.0 copy-start
  137.1 2.1 %copy.13 = bf16[768,512]{1,0:T(8,128)(2,1)} copy(bf16[768,512]{1,0:T(8,128)(2,1)} %get-tuple-element.4) | data formatting | bytes 1572864
  139.2 0.0 copy-done
  139.2 0.9 copy.14
Async XLA Ops:
  137.1 2.1 %copy-start = (bf16[768,512]{1,0:T(8,128)(2,1)S(1)}, bf16[768,512]{1,0:T(8,128)(2,1)}, u32[]{:S(2)}) copy-start(bf16[768,512]{1,0:T(8,128)(2,1)} %get-tuple-element.5) | copy-start | bytes 2359300

commit v2 on v1

--- a/solution.py
+++ b/solution.py
@@ -222,11 +222,10 @@
     value_ref,
     gate_ref,
     taps_ref,
-    out_gate_ref,
     forward_ref,
     inverse_ref,
     attn_ref,
-    hyena_ref,
+    mixed_back,
     near_query,
     near_key,
     near_value,
@@ -242,14 +241,12 @@
     all_value,
     all_gate,
     all_taps,
-    own_out_gate,
     score_buf,
     attn_buf,
     sig_spec,
     tap_spec,
     prod_spec,
     mixed_buf,
-    mixed_back,
     send_sem,
     recv_sem,
     local_sem,
@@ -263,7 +260,6 @@
     half_cols = pl.ds(half * width, width * (groups - half))
     blocks = length // block
     per_row = rows // block
-    reach = KV_REACH * per_row
     me = lax.axis_index("ctx")
     lower = me < half
 
@@ -383,8 +379,6 @@
         source, target = inbound(kind, 0)
         local[kind] = pltpu.make_async_copy(source, target, local_sem.at[kind])
         local[kind].start()
-    gate_copy = pltpu.make_async_copy(out_gate_ref, own_out_gate, local_sem.at[5])
-    gate_copy.start()
 
     def arrive(kind):
         local[kind].wait()
@@ -398,47 +392,53 @@
         starts.append(total)
         total = total + docs_ref[doc]
 
-    def query_tile(tile, query, key_of, value_of):
-        low = jnp.maximum(tile - reach, 0)
-        row_pos = lax.broadcasted_iota(jnp.int32, (block, width), 0) + tile * block
+    def query_tile(group, at, query, key_of, value_of):
+        first = jnp.maximum(group - KV_REACH, 0)
+        row_pos = lax.broadcasted_iota(jnp.int32, (block, width), 0) + (group * rows + at * block)
         row_start = jnp.zeros((block, width), jnp.int32)
         for start in starts:
             row_start = jnp.where(row_pos >= start, start, row_start)
         row_pos = row_pos[:, :1]
         row_start = row_start[:, :1]
-        lane_pos = lax.broadcasted_iota(jnp.int32, (block, block), 1)
-
-        def score_step(at, top):
-            key = key_of(pl.ds(pl.multiple_of(at * block, block), block))
+        lane_pos = lax.broadcasted_iota(jnp.int32, (block, rows), 1)
+
+        def score_step(chunk, top, last=False):
             scores = lax.dot_general(
-                query, key, (((1,), (1,)), ((), ())), preferred_element_type=jnp.float32
-            ) * (1.0 / math.sqrt(HEAD_DIM))
-            key_pos = lane_pos + at * block
-            allowed = (key_pos <= row_pos) & (key_pos >= row_start)
+                query,
+                key_of(rows_of(chunk)),
+                (((1,), (1,)), ((), ())),
+                preferred_element_type=jnp.float32,
+            )
+            allowed = lane_pos >= row_start - chunk * rows
+            if last:
+                allowed = allowed & (lane_pos <= row_pos - chunk * rows)
             scores = jnp.where(allowed, scores, masked_score)
-            score_buf[at - low] = scores
-            for part in range(0, block, width):
+            score_buf[chunk - first] = scores
+            for part in range(0, rows, width):
                 top = jnp.maximum(top, scores[:, part : part + width])
             return top
 
-        top = lax.fori_loop(
-            low, tile + 1, score_step, jnp.full((block, width), masked_score, jnp.float32)
-        )
+        top = jnp.full((block, width), masked_score, jnp.float32)
+        top = lax.fori_loop(first, group, score_step, top)
+        top = score_step(group, top, last=True)
         top = jnp.max(top, axis=1, keepdims=True)
 
-        def value_step(at, carried):
+        def value_step(chunk, carried):
             running, weighted = carried
-            value = value_of(pl.ds(pl.multiple_of(at * block, block), block))
-            weight = jnp.exp(score_buf[at - low] - top)
-            for part in range(0, block, width):
+            weight = jnp.exp2(
+                (score_buf[chunk - first] - top) * (math.log2(math.e) / math.sqrt(HEAD_DIM))
+            )
+            for part in range(0, rows, width):
                 running = running + weight[:, part : part + width]
             weighted = weighted + jnp.dot(
-                weight.astype(jnp.bfloat16), value, preferred_element_type=jnp.float32
+                weight.astype(jnp.bfloat16),
+                value_of(rows_of(chunk)),
+                preferred_element_type=jnp.float32,
             )
             return (running, weighted)
 
         zero = jnp.zeros((block, width), jnp.float32)
-        running, weighted = lax.fori_loop(low, tile + 1, value_step, (zero, zero))
+        running, weighted = lax.fori_loop(first, group + 1, value_step, (zero, zero))
         running = jnp.sum(running, axis=1, keepdims=True)
         return (weighted / running).astype(jnp.bfloat16)
 
@@ -470,7 +470,8 @@
             def near_body(at, carry, cols=cols):
                 part = pl.ds(pl.multiple_of(at * block, block), block)
                 attended = query_tile(
-                    me * per_row + at,
+                    me,
+                    at,
                     near_query[part, cols],
                     lambda rows_at: near_key[rows_at, cols],
                     lambda rows_at: near_value[rows_at, cols],
@@ -524,7 +525,8 @@
             tile = group * per_row + at
             part = pl.ds(pl.multiple_of(tile * block, block), block)
             attn_buf[part, :] = query_tile(
-                tile,
+                group,
+                at,
                 all_query[part, :],
                 lambda rows_at: all_key[rows_at, :],
                 lambda rows_at: all_value[rows_at, :],
@@ -611,35 +613,27 @@
     for place, step in enumerate(order):
         group = lax.rem(me + step, groups)
 
-        def inverse_body(at, carry, group=group, step=step):
+        def inverse_body(at, carry, group=group):
             index = group * per_row + at
             mixed = jnp.dot(
                 inverse_buf[...],
                 prod_spec[index].astype(jnp.bfloat16),
                 preferred_element_type=jnp.float32,
             ).astype(jnp.bfloat16)
-            if step == 0:
-                mixed_back[pl.ds(pl.multiple_of(at * block, block), block), cols_of(me)] = mixed
-            else:
-                mixed_buf[pl.ds(pl.multiple_of(index * block, block), block), :] = mixed
+            mixed_buf[pl.ds(pl.multiple_of(index * block, block), block), :] = mixed
             return carry
 
         lax.fori_loop(0, per_row, inverse_body, 0)
         if place > 0:
             mixed_send(order[place - 1])
 
-    gate_copy.wait()
+    own_mixed = pltpu.make_async_copy(
+        mixed_buf.at[rows_of(me), :], mixed_back.at[:, cols_of(me)], local_sem.at[5]
+    )
+    own_mixed.start()
     for step in range(1, groups):
         sends[6, step].wait_recv()
-
-    def final_body(at, carry):
-        part = pl.ds(pl.multiple_of(at * 64, 64), 64)
-        hyena_ref[part, :] = (
-            own_out_gate[part, :].astype(jnp.float32) * mixed_back[part, :].astype(jnp.float32)
-        ).astype(jnp.bfloat16)
-        return carry
-
-    lax.fori_loop(0, rows // 64, final_body, 0)
+    own_mixed.wait()
     own_attn.wait()
     pl.when(lower)(near_out.wait)
     for step in range(1, groups):
@@ -659,22 +653,20 @@
     length = rows * groups
     block = BLOCK
     blocks = length // block
-    reach = KV_REACH * (rows // block)
     forward, inverse = block_tables(block)
     near = groups // 2
     far = (groups - near) * width
     anywhere = pl.BlockSpec(memory_space=pl.ANY)
-    vmem = pl.BlockSpec(memory_space=pltpu.VMEM)
     half = jnp.bfloat16
     full = jnp.float32
-    return pl.pallas_call(
+    attended, mixed = pl.pallas_call(
         fused_kernel,
         out_shape=(
             jax.ShapeDtypeStruct((rows, channels), half),
             jax.ShapeDtypeStruct((rows, channels), half),
         ),
-        in_specs=[pl.BlockSpec(memory_space=pltpu.SMEM)] + [anywhere] * 8,
-        out_specs=(anywhere, vmem),
+        in_specs=[pl.BlockSpec(memory_space=pltpu.SMEM)] + [anywhere] * 7,
+        out_specs=(anywhere, anywhere),
         scratch_shapes=[
             pltpu.VMEM((rows, far), half),
             pltpu.VMEM((near * rows, far), half),
@@ -691,14 +683,12 @@
             pltpu.VMEM((length, width), half),
             pltpu.VMEM((length, width), half),
             pltpu.VMEM((width, length), half),
-            pltpu.VMEM((rows, channels), half),
-            pltpu.VMEM((min(reach + 1, blocks), block, block), full),
+            pltpu.VMEM((min(KV_REACH + 1, groups), block, rows), full),
             pltpu.VMEM((length, width), half),
             pltpu.VMEM((blocks, 2 * block, width), full),
             pltpu.VMEM((blocks, 2 * block, width), full),
             pltpu.VMEM((blocks, 2 * block, width), full),
             pltpu.VMEM((length, width), half),
-            pltpu.VMEM((rows, channels), half),
             pltpu.SemaphoreType.DMA((9, groups)),
             pltpu.SemaphoreType.DMA((9, groups)),
             pltpu.SemaphoreType.DMA((7,)),
@@ -715,10 +705,11 @@
         values,
         in_gate,
         filter_taps,
-        out_gate,
         forward,
         inverse,
     )
+    hyena_out = (out_gate.astype(full) * mixed.astype(full)).astype(half)
+    return (attended, hyena_out)
 
 
 def fits_fused(queries):

time: 140 us -> 127 us (0.907)
  Pallas kernels: 136 us -> 122 us
  other arithmetic: 0 us -> 2.53 us
  local copies, waits for them, and re-layouts: 3.02 us -> 0.88 us
    pallas_call x1, Pallas kernels: 136 us -> 122 us  [fused_body(): pl.pallas_call(fused_kernel, out_shape=(jax.ShapeDtypeStruct((rows, chann...]
    convert_element_type x0 -> x1, other arithmetic: none -> 2.53 us  [fused_body(): hyena_out = (out_gate.astype(full) * mixed.astype(full)).astype(half)]
    unnamed x4 -> x3, local copies, waits for them, and re-layouts: 3.02 us -> 0.88 us
where the time goes in v2:
time: 127 us; the launch traced here: 126 us
  Pallas kernels  122 us (96%)
  other arithmetic  2.53 us (2%)
    pallas_call x1, Pallas kernels, fused_body(): pl.pallas_call(fused_kernel, out_shape=(jax.ShapeDtypeStruct((rows, chann...  122 us

profile of v2, /device:TPU:24, one launch (start us, length us, event | category | flops | bytes accessed | tf_op | source)
XLA Modules:
  0.0 126.4 jit_solution(15715095541640107920)
XLA Ops:
  0.6 122.4 %fused_window.1 = (bf16[768,512]{1,0:T(8,128)(2,1)}, bf16[768,512]{1,0:T(8,128)(2,1)}) custom-call(s32[8]{0:T(128)} %docs_ref.1, bf16[768,512]{1,0:T(8,128)(2,1)} %query_ref.1, bf16[768,512]{1,0:T(8,128)(2,1)} %key_ref.1, bf16[768,512]{1,0:T(8,128)(2,1)} %value_ref.1, bf16[768,512]{1,0:T(8,128)(2,1)} %gate_ref.1, f32[512,768]{1,0:T(8,128)} %taps_ref.1, ...), custom_call_target="tpu_custom_call" | custom-call | tf_op jit(solution)/shard_map/fused_window/pallas_call | solution.py:662
  123.0 0.0 copy-start
  123.0 2.5 %multiply_convert_fusion = bf16[768,512]{1,0:T(8,128)(2,1)} fusion(bf16[768,512]{1,0:T(8,128)(2,1)} %get-tuple-element.5, bf16[768,512]{1,0:T(8,128)(2,1)} %param.14), kind=kLoop, calls=%fused_computation | loop fusion | flops 1572864 | bytes 2359296 | tf_op jit(solution)/shard_map/convert_element_type | solution.py:711
  125.5 0.0 copy-done
  125.6 0.9 copy.12
Async XLA Ops:
  123.0 2.5 %copy-start = (bf16[768,512]{1,0:T(8,128)(2,1)S(1)}, bf16[768,512]{1,0:T(8,128)(2,1)}, u32[]{:S(2)}) copy-start(bf16[768,512]{1,0:T(8,128)(2,1)} %get-tuple-element.8) | copy-start | bytes 2359300

commit v3 on v2

--- a/solution.py
+++ b/solution.py
@@ -1,3 +1,4 @@
+import functools
 import math
 
 import jax
@@ -540,9 +541,24 @@
         if place > 0:
             attn_send(order[place - 1])
 
-    arrive(4)
     own[5].wait()
     own[6].wait()
+    own_attn = pltpu.make_async_copy(
+        attn_buf.at[rows_of(me), :], attn_ref.at[:, cols_of(me)], local_sem.at[6]
+    )
+    own_attn.start()
+    arrive(3)
+
+    def signal_body(at, carry):
+        row0 = pl.multiple_of(at * block, block)
+        arrived = all_gate[pl.ds(row0, block), :]
+        gated = arrived.astype(jnp.float32) * attn_buf[pl.ds(row0, block), :].astype(jnp.float32)
+        ready = (me >= half) & (at < half * per_row)
+        gated = jnp.where(ready, arrived, gated.astype(jnp.bfloat16))
+        sig_spec[at] = jnp.dot(forward_buf[...], gated, preferred_element_type=jnp.float32)
+        return carry
+
+    lax.fori_loop(0, blocks, signal_body, 0)
 
     def tap_body(at, carry):
         col0 = pl.multiple_of(at * block, block)
@@ -554,34 +570,24 @@
         )
         return carry
 
-    lax.fori_loop(0, blocks, tap_body, 0)
-    own_attn = pltpu.make_async_copy(
-        attn_buf.at[rows_of(me), :], attn_ref.at[:, cols_of(me)], local_sem.at[6]
-    )
-    own_attn.start()
-    arrive(3)
-
-    def signal_body(at, carry):
-        row0 = pl.multiple_of(at * block, block)
-        arrived = all_gate[pl.ds(row0, block), :]
-        gated = arrived.astype(jnp.float32) * attn_buf[pl.ds(row0, block), :].astype(jnp.float32)
-        ready = (me >= half) & (at < half * per_row)
-        gated = jnp.where(ready, arrived, gated.astype(jnp.bfloat16))
-        sig_spec[at] = jnp.dot(forward_buf[...], gated, preferred_element_type=jnp.float32)
-        return carry
-
-    lax.fori_loop(0, blocks, signal_body, 0)
+    for step in range(groups):
+        if step == 0:
+            local[4].wait()
+        else:
+            sends[4, step].wait_recv()
+        group = lax.rem(me + groups - step, groups)
+        lax.fori_loop(group * per_row, (group + 1) * per_row, tap_body, 0)
 
     lift = 8
 
-    def product_body(at, carry):
+    def product_body(group, at, carry):
         real = pl.ds(pl.multiple_of(at * lift, lift), lift)
         imag = pl.ds(pl.multiple_of(block + at * lift, lift), lift)
         odd = lax.rem(lax.broadcasted_iota(jnp.int32, (lift, width), 0), 2) == 1
         sign = jnp.where(odd, -1.0, 1.0).astype(jnp.float32)
         tap_real = []
         tap_imag = []
-        for k in range(blocks):
+        for k in range((group + 1) * per_row):
             now_real = tap_spec[k, real, :]
             now_imag = tap_spec[k, imag, :]
             if k > 0:
@@ -589,7 +595,7 @@
                 now_imag = now_imag + sign * tap_spec[k - 1, real, :]
             tap_real.append(now_real)
             tap_imag.append(now_imag)
-        for out in range(blocks):
+        for out in range(group * per_row, (group + 1) * per_row):
             sum_real = jnp.zeros((lift, width), jnp.float32)
             sum_imag = jnp.zeros((lift, width), jnp.float32)
             for j in range(out + 1):
@@ -601,32 +607,37 @@
             prod_spec[out, imag, :] = sum_imag
         return carry
 
-    lax.fori_loop(0, block // lift, product_body, 0)
-
-    def mixed_send(step):
-        peer = lax.rem(me + step, groups)
+    def inverse_body(at, carry):
+        mixed = jnp.dot(
+            inverse_buf[...],
+            prod_spec[at].astype(jnp.bfloat16),
+            preferred_element_type=jnp.float32,
+        ).astype(jnp.bfloat16)
+        mixed_buf[pl.ds(pl.multiple_of(at * block, block), block), :] = mixed
+        return carry
+
+    def mixed_send(group):
+        for step in range(1, groups):
+
+            @pl.when(lax.rem(me + step, groups) == group)
+            def _(step=step):
+                sends[6, step].start()
+
+    for step in range(1, groups):
         sends[6, step] = remote(
-            lambda: (mixed_buf.at[rows_of(peer), :], mixed_back.at[:, cols_of(me)]), 6, step
+            lambda step=step: (
+                mixed_buf.at[rows_of(lax.rem(me + step, groups)), :],
+                mixed_back.at[:, cols_of(me)],
+            ),
+            6,
+            step,
         )
-        sends[6, step].start()
-
-    for place, step in enumerate(order):
-        group = lax.rem(me + step, groups)
-
-        def inverse_body(at, carry, group=group):
-            index = group * per_row + at
-            mixed = jnp.dot(
-                inverse_buf[...],
-                prod_spec[index].astype(jnp.bfloat16),
-                preferred_element_type=jnp.float32,
-            ).astype(jnp.bfloat16)
-            mixed_buf[pl.ds(pl.multiple_of(index * block, block), block), :] = mixed
-            return carry
-
-        lax.fori_loop(0, per_row, inverse_body, 0)
-        if place > 0:
-            mixed_send(order[place - 1])
-
+    for group in range(groups):
+        lax.fori_loop(0, block // lift, functools.partial(product_body, group), 0)
+        if group > 0:
+            mixed_send(group - 1)
+        lax.fori_loop(group * per_row, (group + 1) * per_row, inverse_body, 0)
+    mixed_send(groups - 1)
     own_mixed = pltpu.make_async_copy(
         mixed_buf.at[rows_of(me), :], mixed_back.at[:, cols_of(me)], local_sem.at[5]
     )

time: 127 us -> 127 us (level)
  no operation moved by 1% of the time
where the time goes in v3:
time: 127 us
  Pallas kernels  123 us (97%)
  other arithmetic  2.53 us (2%)
    pallas_call x1, Pallas kernels, fused_body(): pl.pallas_call(fused_kernel, out_shape=(jax.ShapeDtypeStruct((rows, chann...  123 us

profile of v3, /device:TPU:24, one launch (start us, length us, event | category | flops | bytes accessed | tf_op | source)
XLA Modules:
  0.0 126.9 jit_solution(14878986907251827683)
XLA Ops:
  0.6 122.8 %fused_window.1 = (bf16[768,512]{1,0:T(8,128)(2,1)}, bf16[768,512]{1,0:T(8,128)(2,1)}) custom-call(s32[8]{0:T(128)} %docs_ref.1, bf16[768,512]{1,0:T(8,128)(2,1)} %query_ref.1, bf16[768,512]{1,0:T(8,128)(2,1)} %key_ref.1, bf16[768,512]{1,0:T(8,128)(2,1)} %value_ref.1, bf16[768,512]{1,0:T(8,128)(2,1)} %gate_ref.1, f32[512,768]{1,0:T(8,128)} %taps_ref.1, ...), custom_call_target="tpu_custom_call" | custom-call | tf_op jit(solution)/shard_map/fused_window/pallas_call | solution.py:673
  123.5 0.0 copy-start
  123.5 2.5 %multiply_convert_fusion = bf16[768,512]{1,0:T(8,128)(2,1)} fusion(bf16[768,512]{1,0:T(8,128)(2,1)} %get-tuple-element.5, bf16[768,512]{1,0:T(8,128)(2,1)} %param.14), kind=kLoop, calls=%fused_computation | loop fusion | flops 1572864 | bytes 2359296 | tf_op jit(solution)/shard_map/convert_element_type | solution.py:722
  126.0 0.0 copy-done
  126.0 0.9 copy.12
Async XLA Ops:
  123.5 2.5 %copy-start = (bf16[768,512]{1,0:T(8,128)(2,1)S(1)}, bf16[768,512]{1,0:T(8,128)(2,1)}, u32[]{:S(2)}) copy-start(bf16[768,512]{1,0:T(8,128)(2,1)} %get-tuple-element.8) | copy-start | bytes 2359300
